TPU v7x, 32 devices: a whole 2x2x4 slice. The times are simulated.
32 devices in a mesh: tile: 8 (over z, y), slab: 4 (over x, core).
Axes of the slice: x: 2, y: 2, z: 4, core: 2. Of those that a mesh axis runs over, the one named last changes fastest.
Arguments:
- voxel_cell: int32 [12288, 128], P(('tile', 'slab')), may hold values from 0 to 255
- offsets: float32 [12288, 2, 128], P(('tile', 'slab')), may hold values from 0 to 1
- line_center: float32 [12288, 128], P(('tile', 'slab')), may hold values from 0 to 128
- line_width: float32 [12288, 128], P(('tile', 'slab')), may hold values from 1 to 12
- luminosity: float32 [12288, 128], P(('tile', 'slab')), may hold values from 0.3 to 8
- block_rows: int32 [12288], P(('tile', 'slab')), may hold values from 1 to 128, as said below
- block_chan: int32 [12288], P(('tile', 'slab')), may hold values from 0 to 31, as said below
- slot_table: int32 [32, 768], P(('tile', 'slab')), may hold values from -1 to 383, as said below
- beam_width: float32 [4096], P('slab'), may hold values from 0.6 to 3
- spectral_taps: float32 [31], replicated, may hold values from -3 to 3
Outputs:
- sky_cube: float32 [8, 256, 4096], P('tile', None, 'slab')
Inputs may be any that keep to these rules, and one draw needn't show every extreme that they name: `slot_table`: row i lists the blocks of device i: entry j belongs to destination device j // 24, that is field j // 24 // 4 and slab j // 24 % 4, and holds a local block index or -1 for an empty slot. Every local block stands in exactly one entry of its row. In every draw some destination receives 24 blocks from every device. `block_chan`: A block listed for a destination of slab s has its channel block in s * 8 .. (s + 1) * 8 - 1. Rows 0 .. block_rows - 1 of a block are emitters, the others padding.
All inputs are finite; a program needn't handle non-finite values.
Results may differ from a plain program's by a relative error of at most 0.0045.
Values sent between devices are 32-bit elements; how exact they have to be, the bound alone decides.
No kernel may reach another device: no remote copies, remote signals or barrier semaphores. Data moves between devices by JAX's collectives and lax.ppermute only.
A program may use at most 64 MiB of HBM per device.

v0:
```python
import math

import jax
import jax.numpy as jnp
from jax import lax
from jax.sharding import PartitionSpec as P

SIDE = 16
CB = 128
ROWS = 128
TAPS = 31
HALF = 15
NCB = 32


def extended(cells, sides, width):
    for axis, dim in sides:
        count = lax.axis_size(axis)
        ends = count - 1
        head = lax.slice_in_dim(cells, 0, width, axis=dim)
        tail = lax.slice_in_dim(cells, cells.shape[dim] - width, cells.shape[dim], axis=dim)
        cells = jnp.concatenate(
            [
                lax.ppermute(tail, axis, [(i, (i + 1) % count) for i in range(ends)]),
                cells,
                lax.ppermute(head, axis, [((i + 1) % count, i) for i in range(ends)]),
            ],
            axis=dim,
        )
    return cells


def line_weights(centers, widths, bright):
    channel_pos = lax.broadcasted_iota(jnp.float32, (1, 1, CB), 2) + 0.5
    profile = jnp.exp(
        -jnp.square(channel_pos - centers[:, :, None]) / (2.0 * jnp.square(widths[:, :, None]))
    )
    totals = jnp.sum(profile, axis=2, keepdims=True)
    return (bright[:, :, None] * profile / totals).astype(jnp.bfloat16)


def pixel_weights(cell_ids, frac_x, frac_y):
    cell_x = cell_ids // SIDE
    cell_y = cell_ids % SIDE
    targets = lax.broadcasted_iota(jnp.int32, (1, SIDE * SIDE, 1), 1)
    spread = jnp.zeros((cell_ids.shape[0], SIDE * SIDE, cell_ids.shape[1]), jnp.float32)
    for step_x in (0, 1):
        for step_y in (0, 1):
            weight_x = frac_x if step_x else 1.0 - frac_x
            weight_y = frac_y if step_y else 1.0 - frac_y
            target_x = cell_x + step_x
            target_y = cell_y + step_y
            inside = (target_x < SIDE) & (target_y < SIDE)
            target = jnp.where(inside, target_x * SIDE + target_y, -1)
            spread = spread + jnp.where(
                targets == target[:, None, :], (weight_x * weight_y)[:, None, :], 0.0
            )
    return spread.astype(jnp.bfloat16)


def deposit(cell_ids, emitter_props, chan_index, block_count):
    slot_total = cell_ids.shape[0]
    group_size = math.gcd(slot_total, 32)
    turn_count = slot_total // group_size
    stacked = (
        cell_ids.reshape(turn_count, group_size, ROWS),
        emitter_props.reshape(turn_count, group_size, 5, ROWS),
        chan_index.reshape(turn_count, group_size),
    )

    def add_group(cube_sum, pieces):
        group_cells, group_props, group_chan = pieces
        spread = pixel_weights(group_cells, group_props[:, 0], group_props[:, 1])
        line_rows = line_weights(group_props[:, 2], group_props[:, 3], group_props[:, 4])
        block_part = jnp.einsum(
            "gpr,grc->gpc", spread, line_rows, preferred_element_type=jnp.float32
        )
        return (cube_sum.at[group_chan].add(block_part), None)

    start = jnp.zeros((block_count, SIDE * SIDE, CB), jnp.float32)
    return lax.scan(add_group, start, stacked)[0]


def smooth(grid_cube, widths):
    places = lax.broadcasted_iota(jnp.float32, (SIDE, SIDE, 1), 0)
    others = lax.broadcasted_iota(jnp.float32, (SIDE, SIDE, 1), 1)
    kernel = jnp.exp(-jnp.square(places - others) / (2.0 * jnp.square(widths)[None, None, :]))
    kernel = kernel / jnp.sum(kernel, axis=1, keepdims=True)
    along_x = jnp.einsum("xac,ayc->xyc", kernel, grid_cube, precision=lax.Precision.HIGHEST)
    return jnp.einsum("ybc,xbc->xyc", kernel, along_x, precision=lax.Precision.HIGHEST)


def body(
    voxel_cell,
    offsets,
    line_center,
    line_width,
    luminosity,
    block_rows,
    block_chan,
    slot_table,
    beam_width,
    spectral_taps,
):
    tile_count = lax.axis_size("tile")
    slab_count = lax.axis_size("slab")
    slot_list = slot_table[0]
    per_dest = slot_list.shape[0] // (tile_count * slab_count)
    blocks_share = NCB // slab_count
    filled = slot_list >= 0
    picked = jnp.maximum(slot_list, 0)
    row_pos = lax.broadcasted_iota(jnp.int32, (1, ROWS), 1)
    live_rows = (row_pos < block_rows[picked][:, None]) & filled[:, None]
    rounded = lax.optimization_barrier(luminosity[picked].astype(jnp.bfloat16)).astype(jnp.float32)
    bright = jnp.where(live_rows, rounded, 0.0)
    emitter_props = jnp.concatenate(
        [
            offsets[picked],
            line_center[picked][:, None, :],
            line_width[picked][:, None, :],
            bright[:, None, :],
        ],
        axis=1,
    )
    dest_slab = lax.broadcasted_iota(jnp.int32, slot_list.shape, 0) // per_dest % slab_count
    channels = jnp.where(filled, block_chan[picked], dest_slab * blocks_share)
    cell_ids = voxel_cell[picked]
    own_first = lax.axis_index("slab") * blocks_share
    got_cells, got_props, got_chan = (
        lax.all_to_all(
            cell_ids.reshape(tile_count * slab_count, per_dest, ROWS),
            ("tile", "slab"),
            split_axis=0,
            concat_axis=0,
            tiled=True,
        ),
        lax.all_to_all(
            emitter_props.reshape(tile_count * slab_count, per_dest, 5, ROWS),
            ("tile", "slab"),
            split_axis=0,
            concat_axis=0,
            tiled=True,
        ),
        lax.all_to_all(
            channels.reshape(tile_count * slab_count, per_dest),
            ("tile", "slab"),
            split_axis=0,
            concat_axis=0,
            tiled=True,
        ),
    )
    own_cube = deposit(
        got_cells.reshape(-1, ROWS),
        got_props.reshape(-1, 5, ROWS),
        got_chan.reshape(-1) - own_first,
        blocks_share,
    )
    width_dev = blocks_share * CB
    grid_cube = own_cube.transpose(1, 0, 2).reshape(SIDE, SIDE, width_dev)
    beamed = smooth(grid_cube, beam_width).reshape(SIDE * SIDE, width_dev)
    padded = extended(beamed, (("slab", 1),), HALF)
    result = jnp.zeros_like(beamed)
    for tap_index in range(TAPS):
        result = result + spectral_taps[tap_index] * padded[:, tap_index : tap_index + width_dev]
    return result[None]


def solution(mesh):
    placed = (
        P(("tile", "slab"), None),
        P(("tile", "slab"), None, None),
        P(("tile", "slab"), None),
        P(("tile", "slab"), None),
        P(("tile", "slab"), None),
        P(("tile", "slab")),
        P(("tile", "slab")),
        P(("tile", "slab"), None),
        P("slab"),
        P(),
    )
    return jax.shard_map(
        body, mesh=mesh, in_specs=placed, out_specs=P("tile", None, "slab"), check_vma=False
    )
```

profile of v0, /device:TPU:1, one launch (start us, length us, event | category | flops | bytes accessed | tf_op | source)
XLA Modules:
  0.0 566.2 jit_solution(11820933902982739528)
XLA Ops:
  7.1 7.1 %all-to-all-start = ((s32[32,1,24]{2,1,0:T(1,128)}), s32[32,1,24]{2,1,0:T(1,128)S(1)}, u32[]{:S(2)}, u32[]{:S(2)}) async-start(s32[32,1,24]{2,1,0:T(1,128)} %bitcast.12), calls=%async_computation | async-start | bytes 32768 | tf_op jit(solution)/shard_map/all_to_all | solution.py:144
  37.8 42.1 %all-to-all-done.2 = f32[32,24,5,128]{3,1,2,0:T(8,128)S(1)} async-done(((f32[32,24,5,128]{3,1,2,0:T(8,128)}), f32[32,24,5,128]{3,1,2,0:T(8,128)S(1)}, u32[]{:S(2)}, u32[]{:S(2)}) %all-to-all-start.2) | async-done | bytes 1966112 | tf_op jit(solution)/shard_map/all_to_all | solution.py:137
  84.7 15.5 %fusion.27 = f32[16,1024]{0,1:T(8,128)S(1)} fusion(f32[1024]{0:T(1024)S(1)} %multiply_multiply_fusion, f32[16,16]{1,0:T(8,128)S(1)} %multiply_negate_fusion), kind=kLoop, calls=%fused_computation.69 | loop fusion | flops 507904 | bytes 70656 | tf_op jit(solution)/shard_map/reduce_sum | solution.py:88
  101.9 374.2 %while.12 = (s32[]{:T(128)}, f32[8,256,128]{2,1,0:T(8,128)S(1)}, s32[24,32]{1,0:T(8,128)S(1)}, s32[24,32,128]{2,1,0:T(8,128)S(1)}, f32[24,32,5,128]{3,1,0,2:T(8,128)}, /*index=5*/s32[]{:T(128)}) while((s32[]{:T(128)}, f32[8,256,128]{2,1,0:T(8,128)S(1)}, s32[24,32]{1,0:T(8,128)S(1)}, s32[24,32,128]{2,1,0:T(8,128)S(1)}, ...), condition=%wide.region_3.4_spmd, body=%wide.region_0.3_spmd.sunk | while | flops 288628960 | bytes 17500116 | solution.py:81
  111.0 6.4 %scatter_fusion = f32[8,256,128]{2,1,0:T(8,128)S(1)} fusion(f32[8,256,128]{2,1,0:T(8,128)S(1)} %get-tuple-element.214, s32[32]{0:T(128)S(1)} %fusion.141, f32[32,256,128]{2,1,0:T(8,128)} %fusion.143), kind=kCustom, calls=%fused_computation.7.clone.1 | custom fusion | flops 1048576 | bytes 12583040 | tf_op jit(solution)/shard_map/while/body/eval_jaxpr/scatter-add | solution.py:78
  120.3 6.3 %fusion.143 = f32[32,256,128]{2,1,0:T(8,128)} fusion(f32[32,128]{1,0:T(8,128)S(1)} %get-tuple-element.194, s32[32,128]{1,0:T(8,128)S(1)} %get-tuple-element.197, f32[32,128]{1,0:T(8,128)S(1)} %get-tuple-element.198, s32[32,128]{1,0:T(8,128)S(1)} %get-tuple-element.199, f32[32,128]{1,0:T(8,128)S(1)} %get-tuple-element.200, ...), kind=kOutput, calls=%fused_computation.13.clone.1 | convolution fusion | flops 284688384 | bytes 4391424 | tf_op jit(solution)/shard_map/while/body/eval_jaxpr/gpr,grc->gpc/dot_general | solution.py:75
  126.6 6.5 %scatter_fusion = f32[8,256,128]{2,1,0:T(8,128)S(1)} fusion(f32[8,256,128]{2,1,0:T(8,128)S(1)} %get-tuple-element.214, s32[32]{0:T(128)S(1)} %fusion.141, f32[32,256,128]{2,1,0:T(8,128)} %fusion.143), kind=kCustom, calls=%fused_computation.7.clone.1 | custom fusion | flops 1048576 | bytes 12583040 | tf_op jit(solution)/shard_map/while/body/eval_jaxpr/scatter-add | solution.py:78
  135.9 6.3 %fusion.143 = f32[32,256,128]{2,1,0:T(8,128)} fusion(f32[32,128]{1,0:T(8,128)S(1)} %get-tuple-element.194, s32[32,128]{1,0:T(8,128)S(1)} %get-tuple-element.197, f32[32,128]{1,0:T(8,128)S(1)} %get-tuple-element.198, s32[32,128]{1,0:T(8,128)S(1)} %get-tuple-element.199, f32[32,128]{1,0:T(8,128)S(1)} %get-tuple-element.200, ...), kind=kOutput, calls=%fused_computation.13.clone.1 | convolution fusion | flops 284688384 | bytes 4391424 | tf_op jit(solution)/shard_map/while/body/eval_jaxpr/gpr,grc->gpc/dot_general | solution.py:75
  142.2 6.5 %scatter_fusion = f32[8,256,128]{2,1,0:T(8,128)S(1)} fusion(f32[8,256,128]{2,1,0:T(8,128)S(1)} %get-tuple-element.214, s32[32]{0:T(128)S(1)} %fusion.141, f32[32,256,128]{2,1,0:T(8,128)} %fusion.143), kind=kCustom, calls=%fused_computation.7.clone.1 | custom fusion | flops 1048576 | bytes 12583040 | tf_op jit(solution)/shard_map/while/body/eval_jaxpr/scatter-add | solution.py:78
  151.5 6.3 %fusion.143 = f32[32,256,128]{2,1,0:T(8,128)} fusion(f32[32,128]{1,0:T(8,128)S(1)} %get-tuple-element.194, s32[32,128]{1,0:T(8,128)S(1)} %get-tuple-element.197, f32[32,128]{1,0:T(8,128)S(1)} %get-tuple-element.198, s32[32,128]{1,0:T(8,128)S(1)} %get-tuple-element.199, f32[32,128]{1,0:T(8,128)S(1)} %get-tuple-element.200, ...), kind=kOutput, calls=%fused_computation.13.clone.1 | convolution fusion | flops 284688384 | bytes 4391424 | tf_op jit(solution)/shard_map/while/body/eval_jaxpr/gpr,grc->gpc/dot_general | solution.py:75
  157.8 6.4 %scatter_fusion = f32[8,256,128]{2,1,0:T(8,128)S(1)} fusion(f32[8,256,128]{2,1,0:T(8,128)S(1)} %get-tuple-element.214, s32[32]{0:T(128)S(1)} %fusion.141, f32[32,256,128]{2,1,0:T(8,128)} %fusion.143), kind=kCustom, calls=%fused_computation.7.clone.1 | custom fusion | flops 1048576 | bytes 12583040 | tf_op jit(solution)/shard_map/while/body/eval_jaxpr/scatter-add | solution.py:78
  167.1 6.3 %fusion.143 = f32[32,256,128]{2,1,0:T(8,128)} fusion(f32[32,128]{1,0:T(8,128)S(1)} %get-tuple-element.194, s32[32,128]{1,0:T(8,128)S(1)} %get-tuple-element.197, f32[32,128]{1,0:T(8,128)S(1)} %get-tuple-element.198, s32[32,128]{1,0:T(8,128)S(1)} %get-tuple-element.199, f32[32,128]{1,0:T(8,128)S(1)} %get-tuple-element.200, ...), kind=kOutput, calls=%fused_computation.13.clone.1 | convolution fusion | flops 284688384 | bytes 4391424 | tf_op jit(solution)/shard_map/while/body/eval_jaxpr/gpr,grc->gpc/dot_general | solution.py:75
  173.4 6.4 %scatter_fusion = f32[8,256,128]{2,1,0:T(8,128)S(1)} fusion(f32[8,256,128]{2,1,0:T(8,128)S(1)} %get-tuple-element.214, s32[32]{0:T(128)S(1)} %fusion.141, f32[32,256,128]{2,1,0:T(8,128)} %fusion.143), kind=kCustom, calls=%fused_computation.7.clone.1 | custom fusion | flops 1048576 | bytes 12583040 | tf_op jit(solution)/shard_map/while/body/eval_jaxpr/scatter-add | solution.py:78
  182.7 6.3 %fusion.143 = f32[32,256,128]{2,1,0:T(8,128)} fusion(f32[32,128]{1,0:T(8,128)S(1)} %get-tuple-element.194, s32[32,128]{1,0:T(8,128)S(1)} %get-tuple-element.197, f32[32,128]{1,0:T(8,128)S(1)} %get-tuple-element.198, s32[32,128]{1,0:T(8,128)S(1)} %get-tuple-element.199, f32[32,128]{1,0:T(8,128)S(1)} %get-tuple-element.200, ...), kind=kOutput, calls=%fused_computation.13.clone.1 | convolution fusion | flops 284688384 | bytes 4391424 | tf_op jit(solution)/shard_map/while/body/eval_jaxpr/gpr,grc->gpc/dot_general | solution.py:75
  189.0 6.5 %scatter_fusion = f32[8,256,128]{2,1,0:T(8,128)S(1)} fusion(f32[8,256,128]{2,1,0:T(8,128)S(1)} %get-tuple-element.214, s32[32]{0:T(128)S(1)} %fusion.141, f32[32,256,128]{2,1,0:T(8,128)} %fusion.143), kind=kCustom, calls=%fused_computation.7.clone.1 | custom fusion | flops 1048576 | bytes 12583040 | tf_op jit(solution)/shard_map/while/body/eval_jaxpr/scatter-add | solution.py:78
  204.6 6.5 %scatter_fusion = f32[8,256,128]{2,1,0:T(8,128)S(1)} fusion(f32[8,256,128]{2,1,0:T(8,128)S(1)} %get-tuple-element.214, s32[32]{0:T(128)S(1)} %fusion.141, f32[32,256,128]{2,1,0:T(8,128)} %fusion.143), kind=kCustom, calls=%fused_computation.7.clone.1 | custom fusion | flops 1048576 | bytes 12583040 | tf_op jit(solution)/shard_map/while/body/eval_jaxpr/scatter-add | solution.py:78
  213.9 6.3 %fusion.143 = f32[32,256,128]{2,1,0:T(8,128)} fusion(f32[32,128]{1,0:T(8,128)S(1)} %get-tuple-element.194, s32[32,128]{1,0:T(8,128)S(1)} %get-tuple-element.197, f32[32,128]{1,0:T(8,128)S(1)} %get-tuple-element.198, s32[32,128]{1,0:T(8,128)S(1)} %get-tuple-element.199, f32[32,128]{1,0:T(8,128)S(1)} %get-tuple-element.200, ...), kind=kOutput, calls=%fused_computation.13.clone.1 | convolution fusion | flops 284688384 | bytes 4391424 | tf_op jit(solution)/shard_map/while/body/eval_jaxpr/gpr,grc->gpc/dot_general | solution.py:75
  220.2 6.5 %scatter_fusion = f32[8,256,128]{2,1,0:T(8,128)S(1)} fusion(f32[8,256,128]{2,1,0:T(8,128)S(1)} %get-tuple-element.214, s32[32]{0:T(128)S(1)} %fusion.141, f32[32,256,128]{2,1,0:T(8,128)} %fusion.143), kind=kCustom, calls=%fused_computation.7.clone.1 | custom fusion | flops 1048576 | bytes 12583040 | tf_op jit(solution)/shard_map/while/body/eval_jaxpr/scatter-add | solution.py:78
  229.5 6.3 %fusion.143 = f32[32,256,128]{2,1,0:T(8,128)} fusion(f32[32,128]{1,0:T(8,128)S(1)} %get-tuple-element.194, s32[32,128]{1,0:T(8,128)S(1)} %get-tuple-element.197, f32[32,128]{1,0:T(8,128)S(1)} %get-tuple-element.198, s32[32,128]{1,0:T(8,128)S(1)} %get-tuple-element.199, f32[32,128]{1,0:T(8,128)S(1)} %get-tuple-element.200, ...), kind=kOutput, calls=%fused_computation.13.clone.1 | convolution fusion | flops 284688384 | bytes 4391424 | tf_op jit(solution)/shard_map/while/body/eval_jaxpr/gpr,grc->gpc/dot_general | solution.py:75
  235.8 6.4 %scatter_fusion = f32[8,256,128]{2,1,0:T(8,128)S(1)} fusion(f32[8,256,128]{2,1,0:T(8,128)S(1)} %get-tuple-element.214, s32[32]{0:T(128)S(1)} %fusion.141, f32[32,256,128]{2,1,0:T(8,128)} %fusion.143), kind=kCustom, calls=%fused_computation.7.clone.1 | custom fusion | flops 1048576 | bytes 12583040 | tf_op jit(solution)/shard_map/while/body/eval_jaxpr/scatter-add | solution.py:78
  245.1 6.3 %fusion.143 = f32[32,256,128]{2,1,0:T(8,128)} fusion(f32[32,128]{1,0:T(8,128)S(1)} %get-tuple-element.194, s32[32,128]{1,0:T(8,128)S(1)} %get-tuple-element.197, f32[32,128]{1,0:T(8,128)S(1)} %get-tuple-element.198, s32[32,128]{1,0:T(8,128)S(1)} %get-tuple-element.199, f32[32,128]{1,0:T(8,128)S(1)} %get-tuple-element.200, ...), kind=kOutput, calls=%fused_computation.13.clone.1 | convolution fusion | flops 284688384 | bytes 4391424 | tf_op jit(solution)/shard_map/while/body/eval_jaxpr/gpr,grc->gpc/dot_general | solution.py:75
  251.4 6.4 %scatter_fusion = f32[8,256,128]{2,1,0:T(8,128)S(1)} fusion(f32[8,256,128]{2,1,0:T(8,128)S(1)} %get-tuple-element.214, s32[32]{0:T(128)S(1)} %fusion.141, f32[32,256,128]{2,1,0:T(8,128)} %fusion.143), kind=kCustom, calls=%fused_computation.7.clone.1 | custom fusion | flops 1048576 | bytes 12583040 | tf_op jit(solution)/shard_map/while/body/eval_jaxpr/scatter-add | solution.py:78
  260.7 6.3 %fusion.143 = f32[32,256,128]{2,1,0:T(8,128)} fusion(f32[32,128]{1,0:T(8,128)S(1)} %get-tuple-element.194, s32[32,128]{1,0:T(8,128)S(1)} %get-tuple-element.197, f32[32,128]{1,0:T(8,128)S(1)} %get-tuple-element.198, s32[32,128]{1,0:T(8,128)S(1)} %get-tuple-element.199, f32[32,128]{1,0:T(8,128)S(1)} %get-tuple-element.200, ...), kind=kOutput, calls=%fused_computation.13.clone.1 | convolution fusion | flops 284688384 | bytes 4391424 | tf_op jit(solution)/shard_map/while/body/eval_jaxpr/gpr,grc->gpc/dot_general | solution.py:75
  266.9 6.5 %scatter_fusion = f32[8,256,128]{2,1,0:T(8,128)S(1)} fusion(f32[8,256,128]{2,1,0:T(8,128)S(1)} %get-tuple-element.214, s32[32]{0:T(128)S(1)} %fusion.141, f32[32,256,128]{2,1,0:T(8,128)} %fusion.143), kind=kCustom, calls=%fused_computation.7.clone.1 | custom fusion | flops 1048576 | bytes 12583040 | tf_op jit(solution)/shard_map/while/body/eval_jaxpr/scatter-add | solution.py:78
  276.3 6.3 %fusion.143 = f32[32,256,128]{2,1,0:T(8,128)} fusion(f32[32,128]{1,0:T(8,128)S(1)} %get-tuple-element.194, s32[32,128]{1,0:T(8,128)S(1)} %get-tuple-element.197, f32[32,128]{1,0:T(8,128)S(1)} %get-tuple-element.198, s32[32,128]{1,0:T(8,128)S(1)} %get-tuple-element.199, f32[32,128]{1,0:T(8,128)S(1)} %get-tuple-element.200, ...), kind=kOutput, calls=%fused_computation.13.clone.1 | convolution fusion | flops 284688384 | bytes 4391424 | tf_op jit(solution)/shard_map/while/body/eval_jaxpr/gpr,grc->gpc/dot_general | solution.py:75
  282.5 6.4 %scatter_fusion = f32[8,256,128]{2,1,0:T(8,128)S(1)} fusion(f32[8,256,128]{2,1,0:T(8,128)S(1)} %get-tuple-element.214, s32[32]{0:T(128)S(1)} %fusion.141, f32[32,256,128]{2,1,0:T(8,128)} %fusion.143), kind=kCustom, calls=%fused_computation.7.clone.1 | custom fusion | flops 1048576 | bytes 12583040 | tf_op jit(solution)/shard_map/while/body/eval_jaxpr/scatter-add | solution.py:78
  291.9 6.3 %fusion.143 = f32[32,256,128]{2,1,0:T(8,128)} fusion(f32[32,128]{1,0:T(8,128)S(1)} %get-tuple-element.194, s32[32,128]{1,0:T(8,128)S(1)} %get-tuple-element.197, f32[32,128]{1,0:T(8,128)S(1)} %get-tuple-element.198, s32[32,128]{1,0:T(8,128)S(1)} %get-tuple-element.199, f32[32,128]{1,0:T(8,128)S(1)} %get-tuple-element.200, ...), kind=kOutput, calls=%fused_computation.13.clone.1 | convolution fusion | flops 284688384 | bytes 4391424 | tf_op jit(solution)/shard_map/while/body/eval_jaxpr/gpr,grc->gpc/dot_general | solution.py:75
  298.1 6.5 %scatter_fusion = f32[8,256,128]{2,1,0:T(8,128)S(1)} fusion(f32[8,256,128]{2,1,0:T(8,128)S(1)} %get-tuple-element.214, s32[32]{0:T(128)S(1)} %fusion.141, f32[32,256,128]{2,1,0:T(8,128)} %fusion.143), kind=kCustom, calls=%fused_computation.7.clone.1 | custom fusion | flops 1048576 | bytes 12583040 | tf_op jit(solution)/shard_map/while/body/eval_jaxpr/scatter-add | solution.py:78
  307.5 6.3 %fusion.143 = f32[32,256,128]{2,1,0:T(8,128)} fusion(f32[32,128]{1,0:T(8,128)S(1)} %get-tuple-element.194, s32[32,128]{1,0:T(8,128)S(1)} %get-tuple-element.197, f32[32,128]{1,0:T(8,128)S(1)} %get-tuple-element.198, s32[32,128]{1,0:T(8,128)S(1)} %get-tuple-element.199, f32[32,128]{1,0:T(8,128)S(1)} %get-tuple-element.200, ...), kind=kOutput, calls=%fused_computation.13.clone.1 | convolution fusion | flops 284688384 | bytes 4391424 | tf_op jit(solution)/shard_map/while/body/eval_jaxpr/gpr,grc->gpc/dot_general | solution.py:75
  313.7 6.4 %scatter_fusion = f32[8,256,128]{2,1,0:T(8,128)S(1)} fusion(f32[8,256,128]{2,1,0:T(8,128)S(1)} %get-tuple-element.214, s32[32]{0:T(128)S(1)} %fusion.141, f32[32,256,128]{2,1,0:T(8,128)} %fusion.143), kind=kCustom, calls=%fused_computation.7.clone.1 | custom fusion | flops 1048576 | bytes 12583040 | tf_op jit(solution)/shard_map/while/body/eval_jaxpr/scatter-add | solution.py:78
  323.0 6.3 %fusion.143 = f32[32,256,128]{2,1,0:T(8,128)} fusion(f32[32,128]{1,0:T(8,128)S(1)} %get-tuple-element.194, s32[32,128]{1,0:T(8,128)S(1)} %get-tuple-element.197, f32[32,128]{1,0:T(8,128)S(1)} %get-tuple-element.198, s32[32,128]{1,0:T(8,128)S(1)} %get-tuple-element.199, f32[32,128]{1,0:T(8,128)S(1)} %get-tuple-element.200, ...), kind=kOutput, calls=%fused_computation.13.clone.1 | convolution fusion | flops 284688384 | bytes 4391424 | tf_op jit(solution)/shard_map/while/body/eval_jaxpr/gpr,grc->gpc/dot_general | solution.py:75
  329.3 6.4 %scatter_fusion = f32[8,256,128]{2,1,0:T(8,128)S(1)} fusion(f32[8,256,128]{2,1,0:T(8,128)S(1)} %get-tuple-element.214, s32[32]{0:T(128)S(1)} %fusion.141, f32[32,256,128]{2,1,0:T(8,128)} %fusion.143), kind=kCustom, calls=%fused_computation.7.clone.1 | custom fusion | flops 1048576 | bytes 12583040 | tf_op jit(solution)/shard_map/while/body/eval_jaxpr/scatter-add | solution.py:78
  338.6 6.3 %fusion.143 = f32[32,256,128]{2,1,0:T(8,128)} fusion(f32[32,128]{1,0:T(8,128)S(1)} %get-tuple-element.194, s32[32,128]{1,0:T(8,128)S(1)} %get-tuple-element.197, f32[32,128]{1,0:T(8,128)S(1)} %get-tuple-element.198, s32[32,128]{1,0:T(8,128)S(1)} %get-tuple-element.199, f32[32,128]{1,0:T(8,128)S(1)} %get-tuple-element.200, ...), kind=kOutput, calls=%fused_computation.13.clone.1 | convolution fusion | flops 284688384 | bytes 4391424 | tf_op jit(solution)/shard_map/while/body/eval_jaxpr/gpr,grc->gpc/dot_general | solution.py:75
  344.9 6.5 %scatter_fusion = f32[8,256,128]{2,1,0:T(8,128)S(1)} fusion(f32[8,256,128]{2,1,0:T(8,128)S(1)} %get-tuple-element.214, s32[32]{0:T(128)S(1)} %fusion.141, f32[32,256,128]{2,1,0:T(8,128)} %fusion.143), kind=kCustom, calls=%fused_computation.7.clone.1 | custom fusion | flops 1048576 | bytes 12583040 | tf_op jit(solution)/shard_map/while/body/eval_jaxpr/scatter-add | solution.py:78
  354.2 6.3 %fusion.143 = f32[32,256,128]{2,1,0:T(8,128)} fusion(f32[32,128]{1,0:T(8,128)S(1)} %get-tuple-element.194, s32[32,128]{1,0:T(8,128)S(1)} %get-tuple-element.197, f32[32,128]{1,0:T(8,128)S(1)} %get-tuple-element.198, s32[32,128]{1,0:T(8,128)S(1)} %get-tuple-element.199, f32[32,128]{1,0:T(8,128)S(1)} %get-tuple-element.200, ...), kind=kOutput, calls=%fused_computation.13.clone.1 | convolution fusion | flops 284688384 | bytes 4391424 | tf_op jit(solution)/shard_map/while/body/eval_jaxpr/gpr,grc->gpc/dot_general | solution.py:75
  360.5 6.5 %scatter_fusion = f32[8,256,128]{2,1,0:T(8,128)S(1)} fusion(f32[8,256,128]{2,1,0:T(8,128)S(1)} %get-tuple-element.214, s32[32]{0:T(128)S(1)} %fusion.141, f32[32,256,128]{2,1,0:T(8,128)} %fusion.143), kind=kCustom, calls=%fused_computation.7.clone.1 | custom fusion | flops 1048576 | bytes 12583040 | tf_op jit(solution)/shard_map/while/body/eval_jaxpr/scatter-add | solution.py:78
  369.8 6.3 %fusion.143 = f32[32,256,128]{2,1,0:T(8,128)} fusion(f32[32,128]{1,0:T(8,128)S(1)} %get-tuple-element.194, s32[32,128]{1,0:T(8,128)S(1)} %get-tuple-element.197, f32[32,128]{1,0:T(8,128)S(1)} %get-tuple-element.198, s32[32,128]{1,0:T(8,128)S(1)} %get-tuple-element.199, f32[32,128]{1,0:T(8,128)S(1)} %get-tuple-element.200, ...), kind=kOutput, calls=%fused_computation.13.clone.1 | convolution fusion | flops 284688384 | bytes 4391424 | tf_op jit(solution)/shard_map/while/body/eval_jaxpr/gpr,grc->gpc/dot_general | solution.py:75
  376.1 6.5 %scatter_fusion = f32[8,256,128]{2,1,0:T(8,128)S(1)} fusion(f32[8,256,128]{2,1,0:T(8,128)S(1)} %get-tuple-element.214, s32[32]{0:T(128)S(1)} %fusion.141, f32[32,256,128]{2,1,0:T(8,128)} %fusion.143), kind=kCustom, calls=%fused_computation.7.clone.1 | custom fusion | flops 1048576 | bytes 12583040 | tf_op jit(solution)/shard_map/while/body/eval_jaxpr/scatter-add | solution.py:78
  391.7 6.4 %scatter_fusion = f32[8,256,128]{2,1,0:T(8,128)S(1)} fusion(f32[8,256,128]{2,1,0:T(8,128)S(1)} %get-tuple-element.214, s32[32]{0:T(128)S(1)} %fusion.141, f32[32,256,128]{2,1,0:T(8,128)} %fusion.143), kind=kCustom, calls=%fused_computation.7.clone.1 | custom fusion | flops 1048576 | bytes 12583040 | tf_op jit(solution)/shard_map/while/body/eval_jaxpr/scatter-add | solution.py:78
  407.3 6.5 %scatter_fusion = f32[8,256,128]{2,1,0:T(8,128)S(1)} fusion(f32[8,256,128]{2,1,0:T(8,128)S(1)} %get-tuple-element.214, s32[32]{0:T(128)S(1)} %fusion.141, f32[32,256,128]{2,1,0:T(8,128)} %fusion.143), kind=kCustom, calls=%fused_computation.7.clone.1 | custom fusion | flops 1048576 | bytes 12583040 | tf_op jit(solution)/shard_map/while/body/eval_jaxpr/scatter-add | solution.py:78
  422.9 6.4 %scatter_fusion = f32[8,256,128]{2,1,0:T(8,128)S(1)} fusion(f32[8,256,128]{2,1,0:T(8,128)S(1)} %get-tuple-element.214, s32[32]{0:T(128)S(1)} %fusion.141, f32[32,256,128]{2,1,0:T(8,128)} %fusion.143), kind=kCustom, calls=%fused_computation.7.clone.1 | custom fusion | flops 1048576 | bytes 12583040 | tf_op jit(solution)/shard_map/while/body/eval_jaxpr/scatter-add | solution.py:78
  438.5 6.5 %scatter_fusion = f32[8,256,128]{2,1,0:T(8,128)S(1)} fusion(f32[8,256,128]{2,1,0:T(8,128)S(1)} %get-tuple-element.214, s32[32]{0:T(128)S(1)} %fusion.141, f32[32,256,128]{2,1,0:T(8,128)} %fusion.143), kind=kCustom, calls=%fused_computation.7.clone.1 | custom fusion | flops 1048576 | bytes 12583040 | tf_op jit(solution)/shard_map/while/body/eval_jaxpr/scatter-add | solution.py:78
  454.1 6.5 %scatter_fusion = f32[8,256,128]{2,1,0:T(8,128)S(1)} fusion(f32[8,256,128]{2,1,0:T(8,128)S(1)} %get-tuple-element.214, s32[32]{0:T(128)S(1)} %fusion.141, f32[32,256,128]{2,1,0:T(8,128)} %fusion.143), kind=kCustom, calls=%fused_computation.7.clone.1 | custom fusion | flops 1048576 | bytes 12583040 | tf_op jit(solution)/shard_map/while/body/eval_jaxpr/scatter-add | solution.py:78
  469.7 6.5 %scatter_fusion = f32[8,256,128]{2,1,0:T(8,128)S(1)} fusion(f32[8,256,128]{2,1,0:T(8,128)S(1)} %get-tuple-element.214, s32[32]{0:T(128)S(1)} %fusion.141, f32[32,256,128]{2,1,0:T(8,128)} %fusion.143), kind=kCustom, calls=%fused_computation.7.clone.1 | custom fusion | flops 1048576 | bytes 12583040 | tf_op jit(solution)/shard_map/while/body/eval_jaxpr/scatter-add | solution.py:78
  476.9 6.3 %copy.47 = f32[16,16,1024]{0,1,2:T(8,128)} copy(f32[16,16,1024]{2,1,0:T(8,128)S(1)} %reshape.356) | data formatting | bytes 2097152 | tf_op jit(solution)/shard_map/reshape | solution.py:159
  483.2 17.7 %fusion.29 = f32[1024,16,16]{2,1,0:T(8,128)S(1)} fusion(f32[16,16,1024]{0,1,2:T(8,128)} %copy.47, f32[16,1024]{0,1:T(8,128)S(1)} %fusion.27, f32[1024]{0:T(1024)S(1)} %multiply_multiply_fusion, f32[16,16]{1,0:T(8,128)S(1)} %multiply_negate_fusion), kind=kOutput, calls=%fused_computation.98 | convolution fusion | flops 50855936 | bytes 2167808 | tf_op jit(solution)/shard_map/xac,ayc->xyc/dot_general | solution.py:89
  500.9 20.2 %fusion.31 = f32[16,16,1024]{1,0,2:T(8,128)} fusion(f32[16,1024]{0,1:T(8,128)S(1)} %fusion.27, f32[1024]{0:T(1024)S(1)} %multiply_multiply_fusion, f32[16,16]{1,0:T(8,128)S(1)} %multiply_negate_fusion, f32[1024,16,16]{2,1,0:T(8,128)S(1)} %fusion.29), kind=kOutput, calls=%fused_computation.99 | convolution fusion | flops 50855936 | bytes 2167808 | tf_op jit(solution)/shard_map/ybc,xbc->xyc/dot_general | solution.py:90
  534.9 31.3 %fusion.40 = f32[1,256,1024]{2,1,0:T(8,128)} fusion(f32[256,1024]{1,0:T(8,128)S(1)} %bitcast.129, f32[256,15]{1,0:T(8,128)S(1)} %collective-permute-done.1, f32[256,15]{1,0:T(8,128)S(1)} %collective-permute-done, f32[]{:T(128)} %bitcast.53, f32[]{:T(128)} %bitcast.52, f32[]{:T(128)} %bitcast.51, f32[]{:T(128)} %bitcast.50, f32[]{:T(128)} %bitcast.49, ...), kind=kLoop, calls=%fused_computation.133 | loop fusion | flops 23855104 | bytes 2127996 | tf_op jit(solution)/shard_map/broadcast_in_dim | solution.py:165
  (231 shorter events, 169.3 us)
Async XLA Ops:
  0.0 20.9 %copy-start = (f32[384,2,128]{2,1,0:T(2,128)S(1)}, f32[384,2,128]{2,1,0:T(2,128)}, u32[]{:S(2)}) copy-start(f32[384,2,128]{2,1,0:T(2,128)} %param.13) | copy-start | bytes 1179652
  0.0 14.2 %copy-start.5 = (f32[384,128]{1,0:T(8,128)S(1)}, f32[384,128]{1,0:T(8,128)}, u32[]{:S(2)}) copy-start(f32[384,128]{1,0:T(8,128)} %param.16) | copy-start | bytes 589828
  0.0 15.8 %copy-start.1 = (s32[384]{0:T(512)S(1)}, s32[384]{0:T(512)}, u32[]{:S(2)}) copy-start(s32[384]{0:T(512)} %param.17) | copy-start | bytes 4612
  7.1 21.7 %all-to-all-start = ((s32[32,1,24]{2,1,0:T(1,128)}), s32[32,1,24]{2,1,0:T(1,128)S(1)}, u32[]{:S(2)}, u32[]{:S(2)}) async-start(s32[32,1,24]{2,1,0:T(1,128)} %bitcast.12), calls=%async_computation | async-start | bytes 32768 | tf_op jit(solution)/shard_map/all_to_all | solution.py:144
  14.2 9.6 %copy-start.2 = (f32[384,128]{1,0:T(8,128)S(1)}, f32[384,128]{1,0:T(8,128)}, u32[]{:S(2)}) copy-start(f32[384,128]{1,0:T(8,128)} %param.14) | copy-start | bytes 589828
  20.9 4.5 copy-start.3
  27.4 7.3 %copy-start.4 = (s32[384,128]{1,0:T(8,128)S(1)}, s32[384,128]{1,0:T(8,128)}, u32[]{:S(2)}) copy-start(s32[384,128]{1,0:T(8,128)} %param.12) | copy-start | bytes 589828
  28.8 8.2 %copy-start.6 = (f32[31]{0:T(128)S(1)}, f32[31]{0:T(128)}, u32[]{:S(2)}) copy-start(f32[31]{0:T(128)} %param.21) | copy-start | bytes 376
  28.8 8.9 %copy-start.8 = (f32[1024]{0:T(1024)S(1)}, f32[1024]{0:T(1024)}, u32[]{:S(2)}) copy-start(f32[1024]{0:T(1024)} %param.20) | copy-start | bytes 12292
  28.8 51.0 %all-to-all-start.2 = ((f32[32,24,5,128]{3,1,2,0:T(8,128)}), f32[32,24,5,128]{3,1,2,0:T(8,128)S(1)}, u32[]{:S(2)}, u32[]{:S(2)}) async-start(f32[32,24,5,128]{3,1,2,0:T(8,128)} %copy.43), calls=%async_computation.2 | async-start | bytes 3932160 | tf_op jit(solution)/shard_map/all_to_all | solution.py:137
  79.9 21.9 %all-to-all-start.1 = ((s32[32,24,128]{2,1,0:T(8,128)}), s32[32,24,128]{2,1,0:T(8,128)S(1)}, u32[]{:S(2)}, u32[]{:S(2)}) async-start(s32[32,24,128]{2,1,0:T(8,128)} %bitcast.13), calls=%async_computation.1 | async-start | bytes 786432 | tf_op jit(solution)/shard_map/all_to_all | solution.py:130
  521.1 9.6 %copy-start.7 = (f32[31]{0:T(128)S(1)}, f32[31]{0:T(128)}, u32[]{:S(2)}) copy-start(f32[31]{0:T(128)} %param.21) | copy-start | bytes 376
  526.4 5.1 collective-permute-start
  528.6 6.3 %collective-permute-start.1 = (f32[256,15]{1,0:T(8,128)S(1)}, f32[256,15]{1,0:T(8,128)S(1)}, u32[]{:S(2)}, u32[]{:S(2)}) collective-permute-start(f32[256,15]{1,0:T(8,128)S(1)} %get-tuple-element.118), channel_id=1, source_target_pairs={{1,0},{2,1},{3,2},{5,4},{6,5},{7,6},{9,8},{10,9},{11,10},{13,12},{... | collective-permute-start | bytes 46088 | tf_op jit(solution)/shard_map/ppermute | solution.py:26
where the time goes:
time: 570 us; the launch traced here: 566 us
  other arithmetic  250 us (44%)
  matrix products  188 us (33%)
  local copies, waits for them, and re-layouts  58.3 us (10%)
  waiting for transfers between devices  45.6 us (8%)
  starting transfers between devices  22.1 us (4%)
    scatter-add x24, other arithmetic, add_group(): return (cube_sum.at[group_chan].add(block_part), None)  155 us
    dot_general x24, matrix products, add_group(): jnp.einsum('gpr,grc->gpc', spread, line_rows, preferred_element_type=jnp....  150 us
    reduce_sum x24, other arithmetic, line_weights(): totals = jnp.sum(profile, axis=2, keepdims=True)  43.7 us
    all_to_all x1, waiting for transfers between devices, body(): lax.all_to_all(emitter_props.reshape(tile_count * slab_count, per_dest, 5...  42.1 us
    broadcast_in_dim x1, other arithmetic, body(): return result[None]  31.3 us
    squeeze x24, local copies, waits for them, and re-layouts, deposit(): return lax.scan(add_group, start, stacked)[0]  21.6 us
    dot_general x1, matrix products, smooth(): jnp.einsum('ybc,xbc->xyc', kernel, along_x, precision=lax.Precision.HIGHEST)  20.2 us
    dot_general x1, matrix products, smooth(): jnp.einsum('xac,ayc->xyc', kernel, grid_cube, precision=lax.Precision.HIG...  17.7 us
  transfers between devices with their start and end apart: 5, of which 2 were waited for; matrix products, arithmetic and copies ran while one was open for 6% of the time, Pallas kernels for 0%

commit v1 on v0

v1 whole, which is shorter than its diff:
```python
import functools
import math

import jax
import jax.numpy as jnp
from jax import lax
from jax.experimental import pallas as pl
from jax.experimental.pallas import tpu as pltpu
from jax.sharding import PartitionSpec as P

SIDE = 16
PIX = SIDE * SIDE
CB = 128
ROWS = 128
TAPS = 31
HALF = 15
EDGE = 16
NCB = 32
FIELDS = 6
LOG2E = math.log2(math.e)


def chunk_sizes(per_dest):
    count = 3 if per_dest % 3 == 0 else 1
    return [per_dest // count] * count


def padded_rows(rows):
    return -(-rows // 8) * 8


def pack_kernel(sizes, slab_count, share, slot_ref, count_ref, chan_ref, cell_ref, offset_ref, center_ref,
                width_ref, lum_ref, *refs):
    outs, (cell_f, decay, rounded) = refs[: len(sizes)], refs[len(sizes) :]
    dest_count = outs[0].shape[0]
    per_dest = sum(sizes)
    cell_f[...] = cell_ref[...].astype(jnp.float32)
    decay[...] = (-0.5 * LOG2E) / jnp.square(width_ref[...])
    rounded[...] = lum_ref[...].astype(jnp.bfloat16).astype(jnp.float32)
    lane = lax.broadcasted_iota(jnp.int32, (1, ROWS), 1)

    def one_dest(dest, carry):
        first_chan = lax.rem(dest, slab_count) * share
        chan_row = jnp.zeros((1, ROWS), jnp.int32)
        count_row = jnp.zeros((1, ROWS), jnp.int32)
        slot = 0
        for out, size in zip(outs, sizes):
            for place in range(size):
                block = slot_ref[0, dest * per_dest + slot]
                filled = block >= 0
                block = jnp.maximum(block, 0)
                live = jnp.where(filled, count_ref[block], 0)
                chan = jnp.where(filled, chan_ref[block] - first_chan, 0)
                chan_row = jnp.where(lane == slot, chan, chan_row)
                count_row = jnp.where(lane == slot, live, count_row)
                row = place * FIELDS
                here = pl.ds(block, 1)
                out[dest, row : row + 1, :] = cell_f[here, :]
                out[dest, row + 1 : row + 3, :] = offset_ref[pl.ds(2 * block, 2), :]
                out[dest, row + 3 : row + 4, :] = center_ref[here, :]
                out[dest, row + 4 : row + 5, :] = decay[here, :]
                out[dest, row + 5 : row + 6, :] = jnp.where(lane < live, rounded[here, :], 0.0)
                slot += 1
        meta = sizes[0] * FIELDS
        outs[0][dest, meta : meta + 1, :] = chan_row.astype(jnp.float32)
        outs[0][dest, meta + 1 : meta + 2, :] = count_row.astype(jnp.float32)
        return carry

    lax.fori_loop(0, dest_count, one_dest, 0)


def pack(sizes, dest_count, slab_count, share, slot_list, counts, chans, cells, offsets, centers, widths, lums):
    rows = [size * FIELDS for size in sizes]
    rows[0] += 2
    block_total = cells.shape[0]
    smem = pl.BlockSpec(memory_space=pltpu.SMEM)
    vmem = pl.BlockSpec(memory_space=pltpu.VMEM)
    return pl.pallas_call(
        functools.partial(pack_kernel, sizes, slab_count, share),
        out_shape=[jax.ShapeDtypeStruct((dest_count, padded_rows(r), ROWS), jnp.float32) for r in rows],
        in_specs=[smem] * 3 + [vmem] * 5,
        out_specs=[vmem] * len(sizes),
        scratch_shapes=[pltpu.VMEM((block_total, ROWS), jnp.float32)] * 3,
        name="pack",
    )(slot_list, counts, chans, cells, offsets.reshape(block_total * 2, ROWS), centers, widths, lums)


def deposit_kernel(size, first, chan_ref, got_ref, *refs):
    acc = refs[-1]
    if first == 0:
        acc[...] = jnp.zeros_like(acc)
    else:
        acc[...] = refs[0][...]
    source_count = got_ref.shape[0]
    place16 = lax.broadcasted_iota(jnp.int32, (SIDE, ROWS), 0).astype(jnp.float32)
    chan_pos = lax.broadcasted_iota(jnp.int32, (CB, ROWS), 0).astype(jnp.float32) + 0.5

    def hat(cell, frac):
        apart = place16 - cell
        return jnp.where(apart == 0.0, 1.0 - frac, jnp.where(apart == 1.0, frac, 0.0))

    def one_source(source, carry):
        for place in range(size):
            row = place * FIELDS
            cell, frac_x, frac_y, center, decay, bright = (
                got_ref[source, row + field : row + field + 1, :] for field in range(FIELDS)
            )
            cell_x = jnp.floor(cell * (1.0 / SIDE))
            weight_x = hat(cell_x, frac_x)
            weight_y = hat(cell - SIDE * cell_x, frac_y)
            spread = jnp.concatenate(
                [(weight_x[x : x + 1, :] * weight_y).astype(jnp.bfloat16) for x in range(SIDE)], axis=0
            )
            profile = jnp.exp2(jnp.square(chan_pos - center) * decay)
            scale = bright / jnp.sum(profile, axis=0, keepdims=True)
            line = (profile * scale).astype(jnp.bfloat16)
            part = lax.dot_general(
                spread, line, (((1,), (1,)), ((), ())), preferred_element_type=jnp.float32
            )
            chan = chan_ref[source, first + place]
            acc[chan] += part
        return carry

    lax.fori_loop(0, source_count, one_source, 0)


def deposit(size, first, share, chans, got, *held):
    smem = pl.BlockSpec(memory_space=pltpu.SMEM)
    vmem = pl.BlockSpec(memory_space=pltpu.VMEM)
    work = got.shape[0] * size
    return pl.pallas_call(
        functools.partial(deposit_kernel, size, first),
        out_shape=jax.ShapeDtypeStruct((share, PIX, CB), jnp.float32),
        in_specs=[smem, vmem] + [vmem] * len(held),
        out_specs=vmem,
        input_output_aliases={2: 0} if held else {},
        cost_estimate=pl.CostEstimate(
            flops=work * 2 * PIX * CB * ROWS, transcendentals=work * CB * ROWS, bytes_accessed=got.size * 4
        ),
        name="deposit",
    )(chans, got, *held)


def smooth_kernel(acc_ref, width_ref, out_ref):
    decay = (-0.5 * LOG2E) / jnp.square(width_ref[...])
    places = lax.broadcasted_iota(jnp.int32, (SIDE, CB), 0).astype(jnp.float32)
    beam = [jnp.exp2(jnp.square(places - float(v)) * decay) for v in range(SIDE)]
    norm = beam[0]
    for v in range(1, SIDE):
        norm = norm + beam[v]
    inverse = 1.0 / norm
    beam = [b * inverse for b in beam]
    along_x = [None] * SIDE
    for v in range(SIDE):
        plane = acc_ref[0, v * SIDE : (v + 1) * SIDE, :]
        for x in range(SIDE):
            term = beam[v][x : x + 1, :] * plane
            along_x[x] = term if v == 0 else along_x[x] + term
    for x in range(SIDE):
        total = None
        for v in range(SIDE):
            term = beam[v] * along_x[x][v : v + 1, :]
            total = term if v == 0 else total + term
        out_ref[x * SIDE : (x + 1) * SIDE, :] = total


def smooth(acc, widths):
    share = acc.shape[0]
    return pl.pallas_call(
        smooth_kernel,
        out_shape=jax.ShapeDtypeStruct((PIX, share * CB), jnp.float32),
        grid=(share,),
        in_specs=[
            pl.BlockSpec((1, PIX, CB), lambda i: (i, 0, 0)),
            pl.BlockSpec((1, CB), lambda i: (0, i)),
        ],
        out_specs=pl.BlockSpec((PIX, CB), lambda i: (0, i)),
        name="smooth",
    )(acc, widths.reshape(1, -1))


def taps_kernel(taps_ref, cube_ref, before_ref, after_ref, out_ref):
    span = 3 * CB
    apart = lax.broadcasted_iota(jnp.int32, (span, CB), 0) - lax.broadcasted_iota(jnp.int32, (span, CB), 1)
    band = jnp.zeros((span, CB), jnp.float32)
    for k in range(TAPS):
        band = jnp.where(apart == CB - HALF + k, taps_ref[k], band)
    count = cube_ref.shape[1] // CB

    def times(left, right):
        return jnp.dot(left, right, precision=lax.Precision.HIGHEST, preferred_element_type=jnp.float32)

    for i in range(count):
        low, high = max(i - 1, 0), min(i + 2, count)
        total = times(cube_ref[:, low * CB : high * CB], band[(low - i + 1) * CB : (high - i + 1) * CB])
        if i == 0:
            total = total + times(before_ref[...], band[CB - EDGE : CB])
        if i == count - 1:
            total = total + times(after_ref[...], band[2 * CB : 2 * CB + EDGE])
        out_ref[:, i * CB : (i + 1) * CB] = total


def sum_taps(taps, cube, before, after):
    smem = pl.BlockSpec(memory_space=pltpu.SMEM)
    vmem = pl.BlockSpec(memory_space=pltpu.VMEM)
    return pl.pallas_call(
        taps_kernel,
        out_shape=jax.ShapeDtypeStruct(cube.shape, jnp.float32),
        in_specs=[smem, vmem, vmem, vmem],
        out_specs=vmem,
        name="taps",
    )(taps, cube, before, after)


def body(
    voxel_cell,
    offsets,
    line_center,
    line_width,
    luminosity,
    block_rows,
    block_chan,
    slot_table,
    beam_width,
    spectral_taps,
):
    slab_count = lax.axis_size("slab")
    dest_count = lax.axis_size("tile") * slab_count
    per_dest = slot_table.shape[1] // dest_count
    share = NCB // slab_count
    sizes = chunk_sizes(per_dest)
    sent = pack(
        sizes, dest_count, slab_count, share, slot_table, block_rows, block_chan,
        voxel_cell, offsets, line_center, line_width, luminosity,
    )
    got = [
        lax.all_to_all(piece, ("tile", "slab"), split_axis=0, concat_axis=0, tiled=True) for piece in sent
    ]
    chans = got[0][:, sizes[0] * FIELDS, :per_dest].astype(jnp.int32)
    held = ()
    first = 0
    for size, piece in zip(sizes, got):
        held = (deposit(size, first, share, chans, piece, *held),)
        first += size
    cube = smooth(held[0], beam_width)
    ends = slab_count - 1
    before = lax.ppermute(cube[:, -EDGE:], "slab", [(i, i + 1) for i in range(ends)])
    after = lax.ppermute(cube[:, :EDGE], "slab", [(i + 1, i) for i in range(ends)])
    return sum_taps(spectral_taps, cube, before, after)[None]


def solution(mesh):
    placed = (
        P(("tile", "slab"), None),
        P(("tile", "slab"), None, None),
        P(("tile", "slab"), None),
        P(("tile", "slab"), None),
        P(("tile", "slab"), None),
        P(("tile", "slab")),
        P(("tile", "slab")),
        P(("tile", "slab"), None),
        P("slab"),
        P(),
    )
    return jax.shard_map(
        body, mesh=mesh, in_specs=placed, out_specs=P("tile", None, "slab"), check_vma=False
    )
```

time: 570 us -> 136 us (0.24)
  other arithmetic: 250 us -> 0.6 us
  matrix products: 188 us -> 0 us
  Pallas kernels: 0 us -> 66.9 us
  local copies, waits for them, and re-layouts: 58.3 us -> 2.61 us
  blocking collectives: 0 us -> 53.8 us
  waiting for transfers between devices: 45.6 us -> 1.93 us
  starting transfers between devices: 22.1 us -> 9.95 us
    dot_general x26 -> x0, matrix products: 188 us -> none  [the longest x24 150 us: add_group(): jnp.einsum('gpr,grc->gpc', spread, line_rows, preferred_element_type=jnp....]
    scatter-add x24 -> x0, other arithmetic: 155 us -> none  [add_group(): return (cube_sum.at[group_chan].add(block_part), None)]
    pallas_call x0 -> x6, Pallas kernels: none -> 66.9 us  [the longest x3 48.5 us: deposit(): pl.pallas_call(functools.partial(deposit_kernel, size, first), out_shape=...]
    reduce_sum x25 -> x0, other arithmetic: 59.3 us -> none  [the longest x24 43.7 us: line_weights(): totals = jnp.sum(profile, axis=2, keepdims=True)]
    all_to_all x0 -> x2, blocking collectives: none -> 53.8 us  [body(): lax.all_to_all(piece, ('tile', 'slab'), split_axis=0, concat_axis=0, tile...]
    all_to_all x3 -> x1, waiting for transfers between devices: 42.1 us -> 0.01 us  [body(): lax.all_to_all(piece, ('tile', 'slab'), split_axis=0, concat_axis=0, tile...]
    broadcast_in_dim x1 -> x0, other arithmetic: 31.3 us -> none  [body(): return result[None]]
    squeeze x24 -> x0, local copies, waits for them, and re-layouts: 21.6 us -> none  [deposit(): return lax.scan(add_group, start, stacked)[0]]
  transfers between devices with their start and end apart: 5 -> 3, of which waited for: 2 -> 2; matrix products, arithmetic and copies ran while one was open for 6% -> 0% of each run, Pallas kernels for 0% -> 24%
where the time goes in v1:
time: 136 us
  Pallas kernels  66.9 us (49%)
  blocking collectives  53.8 us (40%)
  starting transfers between devices  9.95 us (7%)
  local copies, waits for them, and re-layouts  2.61 us (2%)
  waiting for transfers between devices  1.93 us (1%)
    all_to_all x2, blocking collectives, body(): lax.all_to_all(piece, ('tile', 'slab'), split_axis=0, concat_axis=0, tile...  53.8 us
    pallas_call x3, Pallas kernels, deposit(): pl.pallas_call(functools.partial(deposit_kernel, size, first), out_shape=...  48.5 us
    pallas_call x1, Pallas kernels, smooth(): pl.pallas_call(smooth_kernel, out_shape=jax.ShapeDtypeStruct((PIX, share...  6.72 us
    pallas_call x1, Pallas kernels, pack(): pl.pallas_call(functools.partial(pack_kernel, sizes, slab_count, share),...  6.59 us
    pallas_call x1, Pallas kernels, sum_taps(): pl.pallas_call(taps_kernel, out_shape=jax.ShapeDtypeStruct(cube.shape, jn...  5.03 us
    all_to_all x1, starting transfers between devices, body(): lax.all_to_all(piece, ('tile', 'slab'), split_axis=0, concat_axis=0, tile...  4.39 us
    ppermute x1, starting transfers between devices, body(): lax.ppermute(cube[:, -EDGE:], 'slab', [(i, i + 1) for i in range(ends)])  3.39 us
  transfers between devices with their start and end apart: 3, of which 2 were waited for; matrix products, arithmetic and copies ran while one was open for 0% of the time, Pallas kernels for 24%

profile of v1, /device:TPU:1, one launch (start us, length us, event | category | flops | bytes accessed | tf_op | source)
XLA Modules:
  0.0 135.8 jit_solution(10676074551798955281)
XLA Ops:
  0.0 6.6 %pack.1 = (f32[32,56,128]{2,1,0:T(8,128)}, f32[32,48,128]{2,1,0:T(8,128)}, f32[32,48,128]{2,1,0:T(8,128)}) custom-call(s32[1,768]{1,0:T(1,128)} %slot_ref.1, s32[384]{0:T(512)} %count_ref.1, s32[384]{0:T(512)} %chan_ref.1, s32[384,128]{1,0:T(8,128)} %cell_ref.1, f32[768,128]{1,0:T(8,128)} %bitcast.6, f32[384,128]{1,0:T(8,128)} %center_ref.1, ...), custom_call_target="tpu_custom_call" | custom-call | tf_op jit(solution)/shard_map/pack/pallas_call | solution.py:78
  6.6 0.0 copy-start.1
  6.6 27.4 %all_to_all.15.got_ref = f32[32,48,128]{2,1,0:T(8,128)} all-to-all(f32[32,48,128]{2,1,0:T(8,128)} %get-tuple-element.10), channel_id=1, replica_groups=mesh['tile'=8,'slab'=4] {'tile','slab'}, dimensions={0} | all-to-all | bytes 1572864 | tf_op jit(solution)/shard_map/all_to_all | solution.py:237
  34.0 0.0 copy-done.1
  34.0 26.4 %all_to_all.16.got_ref = f32[32,56,128]{2,1,0:T(8,128)S(1)} all-to-all(f32[32,56,128]{2,1,0:T(8,128)S(1)} %copy-done.1), channel_id=1, replica_groups=mesh['tile'=8,'slab'=4] {'tile','slab'}, dimensions={0} | all-to-all | bytes 1835008 | tf_op jit(solution)/shard_map/all_to_all | solution.py:237
  60.4 0.0 copy-start
  60.4 4.4 %all-to-all-start.1 = ((f32[32,48,128]{2,1,0:T(8,128)}), f32[32,48,128]{2,1,0:T(8,128)S(1)}, u32[]{:S(2)}, u32[]{:S(2)}) async-start(f32[32,48,128]{2,1,0:T(8,128)} %get-tuple-element.9), calls=%async_computation.1 | async-start | bytes 1572864 | tf_op jit(solution)/shard_map/all_to_all | solution.py:237
  64.8 0.6 convert_bitcast_fusion.chan_ref
  65.4 0.0 copy-done
  65.5 16.0 %deposit.3.refs_0_ = f32[8,256,128]{2,1,0:T(8,128)} custom-call(s32[32,24]{1,0:T(8,128)} %convert_bitcast_fusion.chan_ref, f32[32,56,128]{2,1,0:T(8,128)} %copy-done), custom_call_target="tpu_custom_call" | custom-call | flops 2147483648 | bytes 917504 | tf_op jit(solution)/shard_map/deposit/pallas_call | solution.py:131
  81.5 16.3 %deposit.4.refs_0_ = f32[8,256,128]{2,1,0:T(8,128)} custom-call(s32[32,24]{1,0:T(8,128)} %convert_bitcast_fusion.chan_ref, f32[32,48,128]{2,1,0:T(8,128)} %all_to_all.15.got_ref, f32[8,256,128]{2,1,0:T(8,128)} %deposit.3.refs_0_), custom_call_target="tpu_custom_call", output_to_operand_aliasing={{}: (2, {})} | custom-call | flops 2147483648 | bytes 786432 | tf_op jit(solution)/shard_map/deposit/pallas_call | solution.py:131
  97.7 0.0 all-to-all-done.1.got_ref
  97.7 0.0 copy-start.2
  97.7 0.9 copy-done.2
  98.6 16.3 %deposit.5.acc_ref = f32[8,256,128]{2,1,0:T(8,128)} custom-call(s32[32,24]{1,0:T(8,128)} %convert_bitcast_fusion.chan_ref, f32[32,48,128]{2,1,0:T(8,128)} %copy-done.2, f32[8,256,128]{2,1,0:T(8,128)} %deposit.4.refs_0_), custom_call_target="tpu_custom_call", output_to_operand_aliasing={{}: (2, {})} | custom-call | flops 2147483648 | bytes 786432 | tf_op jit(solution)/shard_map/deposit/pallas_call | solution.py:131
  114.9 6.7 %smooth.1.cube_ref = f32[256,1024]{1,0:T(8,128)} custom-call(f32[8,256,128]{2,1,0:T(8,128)} %deposit.5.acc_ref, f32[1,1024]{1,0:T(1,128)} %bitcast.8), custom_call_target="tpu_custom_call" | custom-call | tf_op jit(solution)/shard_map/smooth/pallas_call | solution.py:169
  121.6 1.1 fusion
  122.7 2.2 %collective-permute-start.1 = (f32[256,16]{1,0:T(8,128)S(1)}, f32[256,16]{1,0:T(8,128)S(1)}, u32[]{:S(2)}, u32[]{:S(2)}) collective-permute-start(f32[256,16]{1,0:T(8,128)S(1)} %get-tuple-element.11), channel_id=1, source_target_pairs={{1,0},{2,1},{3,2},{5,4},{6,5},{7,6},{9,8},{10,9},{11,10},{13,12},{... | collective-permute-start | bytes 49160 | tf_op jit(solution)/shard_map/ppermute | solution.py:248
  124.8 3.4 %collective-permute-start = (f32[256,16]{1,0:T(8,128)S(1)}, f32[256,16]{1,0:T(8,128)S(1)}, u32[]{:S(2)}, u32[]{:S(2)}) collective-permute-start(f32[256,16]{1,0:T(8,128)S(1)} %get-tuple-element.12), channel_id=1, source_target_pairs={{0,1},{1,2},{2,3},{4,5},{5,6},{6,7},{8,9},{9,10},{10,11},{12,13},{... | collective-permute-start | bytes 49160 | tf_op jit(solution)/shard_map/ppermute | solution.py:247
  128.2 0.7 collective-permute-done.1.after_ref
  128.9 0.0 copy-start.3
  128.9 1.2 collective-permute-done.before_ref
  130.2 0.0 copy-done.3
  130.2 0.0 copy-start.4
  130.2 0.7 copy-done.4
  130.8 5.0 %taps.1 = f32[256,1024]{1,0:T(8,128)} custom-call(f32[31]{0:T(128)} %taps_ref.1, f32[256,1024]{1,0:T(8,128)} %smooth.1.cube_ref, f32[256,16]{1,0:T(8,128)} %copy-done.4, f32[256,16]{1,0:T(8,128)} %copy-done.3), custom_call_target="tpu_custom_call" | custom-call | tf_op jit(solution)/shard_map/taps/pallas_call | solution.py:206
  (1 shorter events, 0.0 us)
Async XLA Ops:
  6.6 27.4 %copy-start.1 = (f32[32,56,128]{2,1,0:T(8,128)S(1)}, f32[32,56,128]{2,1,0:T(8,128)}, u32[]{:S(2)}) copy-start(f32[32,56,128]{2,1,0:T(8,128)} %get-tuple-element.8) | copy-start | bytes 2752516
  60.4 5.0 %copy-start = (f32[32,56,128]{2,1,0:T(8,128)}, f32[32,56,128]{2,1,0:T(8,128)S(1)}, u32[]{:S(2)}) copy-start(f32[32,56,128]{2,1,0:T(8,128)S(1)} %all_to_all.16.got_ref) | copy-start | bytes 2752516
  60.4 37.3 %all-to-all-start.1 = ((f32[32,48,128]{2,1,0:T(8,128)}), f32[32,48,128]{2,1,0:T(8,128)S(1)}, u32[]{:S(2)}, u32[]{:S(2)}) async-start(f32[32,48,128]{2,1,0:T(8,128)} %get-tuple-element.9), calls=%async_computation.1 | async-start | bytes 1572864 | tf_op jit(solution)/shard_map/all_to_all | solution.py:237
  97.7 0.9 copy-start.2
  122.7 6.3 %collective-permute-start.1 = (f32[256,16]{1,0:T(8,128)S(1)}, f32[256,16]{1,0:T(8,128)S(1)}, u32[]{:S(2)}, u32[]{:S(2)}) collective-permute-start(f32[256,16]{1,0:T(8,128)S(1)} %get-tuple-element.11), channel_id=1, source_target_pairs={{1,0},{2,1},{3,2},{5,4},{6,5},{7,6},{9,8},{10,9},{11,10},{13,12},{... | collective-permute-start | bytes 49160 | tf_op jit(solution)/shard_map/ppermute | solution.py:248
  124.8 5.3 %collective-permute-start = (f32[256,16]{1,0:T(8,128)S(1)}, f32[256,16]{1,0:T(8,128)S(1)}, u32[]{:S(2)}, u32[]{:S(2)}) collective-permute-start(f32[256,16]{1,0:T(8,128)S(1)} %get-tuple-element.12), channel_id=1, source_target_pairs={{0,1},{1,2},{2,3},{4,5},{5,6},{6,7},{8,9},{9,10},{10,11},{12,13},{... | collective-permute-start | bytes 49160 | tf_op jit(solution)/shard_map/ppermute | solution.py:247
  128.9 1.2 copy-start.3
  130.2 0.7 copy-start.4
